TPU v7x, 32 devices: a whole 2x2x4 slice. The times are simulated.
32 devices in a mesh: grp: 1, wide: 8 (over z, y), narrow: 4 (over x, core).
Axes of the slice: x: 2, y: 2, z: 4, core: 2. Of those that a mesh axis runs over, the one named last changes fastest.
Arguments:
- vectors: bfloat16 [512, 2, 3, 16, 512], P('grp', None, None, 'wide', 'narrow'), may hold values from -6 to 6
- links: float32 [3, 2, 3, 3, 16, 512], P('grp', None, None, None, 'wide', 'narrow'), may hold values from -4 to 4
- directions: int32 [3], replicated, may hold values from 0 to 2, each once
- peram: bfloat16 [2, 512, 256], P('grp', 'wide', 'narrow'), may hold values from -0.1875 to 0.1875
Outputs:
- elementals: float32 [3, 2, 512, 512], P('grp', None, 'wide')
- products: float32 [3, 2, 512, 256], P('grp', None, 'wide', 'narrow')
All inputs are finite; a program needn't handle non-finite values.
Results may differ from a plain program's by a relative error of at most 0.004.
Values may be sent and summed in bfloat16 or wider, within the bound.
A program may use at most 64 MiB of HBM per device.

v0:
```python
import math
import jax
import jax.numpy as jnp
from jax import lax
from jax.sharding import PartitionSpec as P

LZ = 16


def from_behind(x, axis, by):
    length = lax.axis_size(axis)
    return lax.ppermute(x, axis, [(i, (i + by) % length) for i in range(length)])


def covariant_product(link_field, shifted):
    link_real = link_field[0][None]
    link_imag = link_field[1][None]
    vec_real = shifted[:, 0][:, None]
    vec_imag = shifted[:, 1][:, None]
    out_real = jnp.sum(link_real * vec_real - link_imag * vec_imag, axis=2)
    out_imag = jnp.sum(link_real * vec_imag + link_imag * vec_real, axis=2)
    return jnp.stack([out_real, out_imag], 1).astype(jnp.bfloat16)


def on_device(vectors, links, directions, peram):
    vec_count = vectors.shape[0]
    plane_count = vectors.shape[3]
    row_length = vectors.shape[4]
    direction_count = directions.shape[0]
    col_count = peram.shape[2]
    wide_count = lax.axis_size("wide")
    narrow_count = lax.axis_size("narrow")
    norm_factor = 1.0 / math.sqrt(12.0 * plane_count * wide_count * row_length * narrow_count)
    next_first = from_behind(vectors[:, :, :, 0:1], "wide", -1)
    along_first = jnp.concatenate([vectors[:, :, :, 1:], next_first], 3)
    next_second = from_behind(vectors[:, :, :, :, 0:LZ], "narrow", -1)
    along_second = jnp.concatenate([vectors[:, :, :, :, LZ:], next_second], 4)
    along_third = jnp.roll(
        vectors.reshape(vec_count, 2, 3, plane_count, row_length // LZ, LZ), -1, axis=5
    ).reshape(vectors.shape)
    rotated = jnp.concatenate([-vectors[:, 1:2], vectors[:, 0:1]], 1)
    left_block = jnp.concatenate(
        [vectors.reshape(vec_count, -1), rotated.reshape(vec_count, -1)], 0
    )
    partials = []
    for slot_index in range(direction_count):
        chosen = directions[slot_index]
        shifted = jnp.where(
            chosen == 0, along_first, jnp.where(chosen == 1, along_second, along_third)
        )
        link_field = jnp.where(chosen == 0, links[0], jnp.where(chosen == 1, links[1], links[2]))
        product = covariant_product(link_field, shifted).reshape(vec_count, -1)
        partials.append(
            lax.dot_general(
                left_block, product, (((1,), (1,)), ((), ())), preferred_element_type=jnp.float32
            )
        )
    halves = jnp.stack(partials).reshape(direction_count, 2, vec_count, vec_count) * norm_factor
    real_part = halves[:, 0]
    imag_part = halves[:, 1]
    local_terms = jnp.stack(
        [real_part - jnp.swapaxes(real_part, 1, 2), imag_part + jnp.swapaxes(imag_part, 1, 2)], 1
    )
    rows_here = vec_count // wide_count
    thin_rows = lax.psum_scatter(local_terms, ("wide", "narrow"), scatter_dimension=2, tiled=True)
    elementals = lax.all_gather(thin_rows, "narrow", axis=2, tiled=True)
    elem_low = elementals.astype(jnp.bfloat16)
    real_rows = elem_low[:, 0]
    imag_rows = elem_low[:, 1]
    piece = lax.all_gather(peram, "wide", axis=1, tiled=True)
    width = piece.shape[1]
    left_part = jnp.concatenate([real_rows, imag_rows], 2).reshape(-1, 2 * width)
    right_part = jnp.concatenate(
        [jnp.concatenate([piece[0], piece[1]], 1), jnp.concatenate([-piece[1], piece[0]], 1)], 0
    )
    summed = jnp.dot(left_part, right_part, preferred_element_type=jnp.float32)
    products = summed.reshape(direction_count, rows_here, 2, col_count).transpose(0, 2, 1, 3)
    return (elementals, products)


def solution(mesh):
    placed = (
        P("grp", None, None, "wide", "narrow"),
        P("grp", None, None, None, "wide", "narrow"),
        P(),
        P("grp", "wide", "narrow"),
    )
    return jax.shard_map(
        on_device,
        mesh=mesh,
        in_specs=placed,
        out_specs=(P("grp", None, "wide", None), P("grp", None, "wide", "narrow")),
        check_vma=False,
    )
```

profile of v0, /device:TPU:0, one launch (start us, length us, event | category | flops | bytes accessed | tf_op | source)
XLA Modules:
  0.0 246.1 jit_solution(10593543814689281994)
XLA Ops:
  7.2 3.6 %copy.27 = bf16[512,2,3,2,128]{0,4,3,2,1:T(8,128)(2,1)S(1)} copy(bf16[512,2,3,2,128]{4,3,2,1,0:T(2,128)(2,1)} %param.4) | data formatting | bytes 3145728 | tf_op args[0]
  12.1 6.0 %collective-permute-start = (bf16[512,2,3,1,128]{0,4,3,2,1:T(8,128)(2,1)}, bf16[512,2,3,1,128]{0,4,3,2,1:T(8,128)(2,1)}, u32[]{:S(2)}, u32[]{:S(2)}) collective-permute-start(bf16[512,2,3,1,128]{0,4,3,2,1:T(8,128)(2,1)} %get-tuple-element.28), channel_id=1, source_target_pairs={{0,28},{4,0},{8,4},{12,8},{16,12},{20,16},{24,20},{28,24},{1,29},{... | collective-permute-start | bytes 2359304 | tf_op jit(solution)/shard_map/ppermute | solution.py:12
  25.2 3.2 %pad_maximum_fusion.2 = bf16[512,2,3,2,128]{4,3,2,1,0:T(2,128)(2,1)} fusion(bf16[512,1,3,2,128]{4,3,2,1,0:T(2,128)(2,1)S(1)} %get-tuple-element.30, bf16[512,1,3,2,128]{4,3,2,1,0:T(2,128)(2,1)S(1)} %get-tuple-element.29), kind=kLoop, calls=%fused_computation.17 | loop fusion | flops 786432 | bytes 3145728 | tf_op jit(solution)/shard_map/concatenate | solution.py:41
  29.0 1.7 pad_maximum_fusion.5
  31.9 1.5 reshape.106
  36.6 3.4 %pad_maximum_fusion.1 = bf16[1024,1536]{1,0:T(8,128)(2,1)} fusion(bf16[512,1536]{1,0:T(8,128)(2,1)} %reshape.107, bf16[512,1536]{1,0:T(8,128)(2,1)S(1)} %copy-done.3), kind=kLoop, calls=%fused_computation.9 | loop fusion | flops 6291456 | bytes 6291456 | tf_op jit(solution)/shard_map/concatenate | solution.py:42
  40.7 3.5 %fusion.2 = (bf16[512,2,3,2,128]{0,4,3,2,1:T(8,128)(2,1)S(1)}, bf16[512,2,3,2,128]{0,4,3,2,1:T(8,128)(2,1)}, bf16[512,2,3,2,128]{0,4,3,2,1:T(8,128)(2,1)}) fusion(bf16[512,2,3,2,8,16]{0,5,4,3,2,1:T(8,128)(2,1)S(1)} %copy-done.5, pred[]{:T(512)} %bitcast.2, pred[]{:T(512)} %bitcast.1, bf16[512,2,3,2,16]{0,4,3,2,1:T(8,128)(2,1)S(1)} %collective-permute-done.1, ...), kind=kLoop, calls=%fused_computation.27 | loop fusion | flops 11010048 | bytes 9437190 | tf_op jit(solution)/shard_map/jit(_where)/select_n | solution.py:48
  44.2 1.6 fusion.10
  46.3 1.9 copy.33
  49.8 1.6 copy.34
  51.4 1.5 reshape.117
  52.9 4.4 %fusion.6 = (f32[512,3,2,128]{0,3,2,1:T(8,128)S(1)}, f32[512,3,2,128]{0,3,2,1:T(8,128)S(1)}, f32[512,3,2,128]{0,3,2,1:T(8,128)}, f32[512,3,2,128]{0,3,2,1:T(8,128)}) fusion(bf16[512,2,3,2,128]{0,4,3,2,1:T(8,128)(2,1)} %get-tuple-element.20, bf16[512,2,3,2,128]{0,4,3,2,1:T(8,128)(2,1)} %get-tuple-element.19), kind=kLoop, calls=%fused_computation.34 | loop fusion | flops 1572864 | bytes 9437184 | tf_op jit(solution)/shard_map/mul | solution.py:20
  57.4 3.1 %copy.35 = f32[512,3,2,128]{3,0,2,1:T(8,128)} copy(f32[512,3,2,128]{0,3,2,1:T(8,128)} %get-tuple-element.48) | data formatting | bytes 3145728 | tf_op jit(solution)/shard_map/mul | solution.py:20
  60.5 3.1 %copy.36 = f32[512,3,2,128]{3,0,2,1:T(8,128)} copy(f32[512,3,2,128]{0,3,2,1:T(8,128)} %get-tuple-element.47) | data formatting | bytes 3145728 | tf_op jit(solution)/shard_map/mul | solution.py:20
  63.6 3.3 %subtract_reduce_fusion.1 = (bf16[512,3,2,128]{3,0,2,1:T(8,128)(2,1)S(1)}, bf16[512,3,2,128]{3,0,2,1:T(8,128)(2,1)S(1)}) fusion(f32[512,3,2,128]{3,0,2,1:T(8,128)} %copy.36, f32[3,3,2,128]{3,2,1,0:T(2,128)S(1)} %copy-done.15, f32[512,3,2,128]{3,0,2,1:T(8,128)} %copy.35, f32[3,3,2,128]{3,2,1,0:T(2,128)S(1)} %copy-done.16), kind=kLoop, calls=%fused_computation.5 | loop fusion | flops 8650752 | bytes 4737024 | tf_op jit(solution)/shard_map/reduce_sum | solution.py:20
  67.0 2.8 %copy.37 = bf16[512,2,3,2,128]{4,3,2,1,0:T(2,128)(2,1)} copy(bf16[512,2,3,2,128]{4,0,3,2,1:T(8,128)(2,1)S(1)} %pad_maximum_fusion.7) | data formatting | bytes 3145728 | tf_op jit(solution)/shard_map/stack | solution.py:22
  69.8 4.9 %reshape.118 = bf16[512,1536,1]{1,0,2:T(8,128)(2,1)} reshape(bf16[512,2,3,2,128]{4,3,2,1,0:T(2,128)(2,1)} %copy.37) | data formatting | bytes 3145728 | tf_op jit(solution)/shard_map/convert_element_type | solution.py:22
  74.7 5.7 %convolution_bitcast_fusion.2 = f32[1,2,512,512]{3,2,1,0:T(8,128)} fusion(bf16[2,512,1536]{2,1,0:T(8,128)(2,1)} %bitcast.135, bf16[512,1536,1]{1,0,2:T(8,128)(2,1)} %reshape.117), kind=kOutput, calls=%fused_computation.16 | convolution fusion | flops 1610612736 | bytes 6815744 | tf_op jit(solution)/shard_map/dot_general | solution.py:54
  80.4 3.2 %convolution_bitcast_fusion.1 = f32[1,2,512,512]{3,2,1,0:T(8,128)} fusion(bf16[2,512,1536]{2,1,0:T(8,128)(2,1)S(1)} %bitcast.137, bf16[512,1536,1]{1,0,2:T(8,128)(2,1)S(1)} %copy-done.11), kind=kOutput, calls=%fused_computation.15 | convolution fusion | flops 1610612736 | bytes 6815744 | tf_op jit(solution)/shard_map/dot_general | solution.py:54
  83.6 1.6 copy.38
  85.2 1.7 copy.39
  86.9 2.8 %subtract_reduce_fusion = (bf16[512,3,2,128]{3,0,2,1:T(8,128)(2,1)S(1)}, bf16[512,3,2,128]{3,0,2,1:T(8,128)(2,1)S(1)}) fusion(f32[512,3,2,128]{3,0,2,1:T(8,128)} %copy.39, f32[3,3,2,128]{3,2,1,0:T(2,128)S(1)} %copy-done.14, f32[512,3,2,128]{3,0,2,1:T(8,128)S(1)} %copy-done.4, f32[3,3,2,128]{3,2,1,0:T(2,128)S(1)} %get-tuple-element.42), kind=kLoop, calls=%fused_computation.3 | loop fusion | flops 8650752 | bytes 4737024 | tf_op jit(solution)/shard_map/reduce_sum | solution.py:20
  89.9 1.6 copy.40
  92.2 3.9 %convolution_bitcast_fusion = f32[1,2,512,512]{3,2,1,0:T(8,128)S(1)} fusion(bf16[2,512,1536]{2,1,0:T(8,128)(2,1)} %bitcast.136, bf16[512,1536,1]{1,0,2:T(8,128)(2,1)S(1)} %reshape.119), kind=kOutput, calls=%fused_computation.14 | convolution fusion | flops 1610612736 | bytes 6815744 | tf_op jit(solution)/shard_map/dot_general | solution.py:54
  97.4 3.7 %fusion.15 = (f32[3,1,512,512]{3,2,1,0:T(8,128)}, f32[3,512,512]{2,1,0:T(8,128)}) fusion(f32[3,2,512,512]{3,2,1,0:T(8,128)S(1)} %maximum_multiply_fusion), kind=kLoop, calls=%fused_computation.69 | loop fusion | bytes 12582912 | tf_op jit(solution)/shard_map/slice | solution.py:59
  101.9 2.4 copy.43
  104.3 3.5 %copy.47 = f32[3,1,512,512]{2,3,0,1:T(8,128)} copy(f32[3,1,512,512]{3,2,1,0:T(8,128)} %get-tuple-element.16) | data formatting | bytes 6291456
  107.8 5.3 %fusion = (f32[3,1,512,512]{3,2,0,1:T(8,128)S(1)}, f32[3,1,512,512]{3,2,0,1:T(8,128)S(1)}) fusion(f32[3,1,512,512]{2,3,0,1:T(8,128)} %copy.47, f32[3,2,512,512]{3,2,1,0:T(8,128)} %copy-done, f32[3,512,512]{1,2,0:T(8,128)S(1)} %copy.43), kind=kLoop, calls=%fused_computation.11 | loop fusion | flops 1572864 | bytes 18874368 | tf_op jit(solution)/shard_map/stack | solution.py:61
  113.2 3.4 %pad_maximum_fusion = f32[3,2,512,512]{3,2,0,1:T(8,128)} fusion(f32[3,1,512,512]{3,2,0,1:T(8,128)S(1)} %get-tuple-element.15, f32[3,1,512,512]{3,2,0,1:T(8,128)S(1)} %get-tuple-element.14), kind=kLoop, calls=%fused_computation.1 | loop fusion | flops 1572864 | bytes 12582912 | tf_op jit(solution)/shard_map/stack | solution.py:61
  117.3 30.8 %all_gather.7 = bf16[2,512,64]{2,1,0:T(8,128)(2,1)S(1)} all-gather(bf16[2,64,64]{2,1,0:T(8,128)(2,1)S(1)} %copy-done.19), channel_id=1, replica_groups=mesh['grp'=1,'wide'=8,'narrow'=4] {'wide'}, dimensions={1}, use_global_device_ids=true | all-gather | bytes 147456 | tf_op jit(solution)/shard_map/all_gather | solution.py:70
  148.4 79.9 %reduce-scatter.2.cloned.1.call-done = f32[3,2,16,512]{3,2,0,1:T(8,128)} async-done(((f32[3,2,512,512]{3,2,0,1:T(8,128)}), f32[3,2,16,512]{3,2,0,1:T(8,128)}) %reduce-scatter.2.cloned.1.call-update) | async-done | bytes 196624 | tf_op jit(solution)/shard_map/reduce_scatter | solution.py:65
  228.4 8.9 %all_gather.6 = f32[3,2,64,512]{3,2,0,1:T(8,128)S(1)} all-gather(f32[3,2,16,512]{3,2,0,1:T(8,128)} %reduce-scatter.2.cloned.1.call-done), channel_id=1, replica_groups=mesh['grp'=1,'wide'=8,'narrow'=4] {'narrow'}, dimensions={2}, use_global_device_ids=true | all-gather | bytes 983040 | tf_op jit(solution)/shard_map/all_gather | solution.py:66
  (73 shorter events, 18.5 us)
Async XLA Ops:
  7.2 221.2 %reduce-scatter.2.cloned.1.call-start = ((), (), s32[]{:S(2)}) async-start(), calls=%async_computation.1 | async-start | bytes 6488064 | tf_op jit(solution)/shard_map/reduce_scatter | solution.py:65
  12.1 7.7 %copy-start.20 = (s32[3]{0:T(128)S(1)}, s32[3]{0:T(128)}, u32[]{:S(2)}) copy-start(s32[3]{0:T(128)} %param.6) | copy-start | bytes 40
  12.1 11.9 %copy-start.1 = (bf16[512,2,3,2,128]{4,3,2,1,0:T(2,128)(2,1)S(1)}, bf16[512,2,3,2,128]{4,3,2,1,0:T(2,128)(2,1)}, u32[]{:S(2)}) copy-start(bf16[512,2,3,2,128]{4,3,2,1,0:T(2,128)(2,1)} %param.4) | copy-start | bytes 4718596
  12.1 28.5 %collective-permute-start = (bf16[512,2,3,1,128]{0,4,3,2,1:T(8,128)(2,1)}, bf16[512,2,3,1,128]{0,4,3,2,1:T(8,128)(2,1)}, u32[]{:S(2)}, u32[]{:S(2)}) collective-permute-start(bf16[512,2,3,1,128]{0,4,3,2,1:T(8,128)(2,1)} %get-tuple-element.28), channel_id=1, source_target_pairs={{0,28},{4,0},{8,4},{12,8},{16,12},{20,16},{24,20},{28,24},{1,29},{... | collective-permute-start | bytes 2359304 | tf_op jit(solution)/shard_map/ppermute | solution.py:12
  18.2 22.5 %collective-permute-start.1 = (bf16[512,2,3,2,16]{0,4,3,2,1:T(8,128)(2,1)S(1)}, bf16[512,2,3,2,16]{0,4,3,2,1:T(8,128)(2,1)S(1)}, u32[]{:S(2)}, u32[]{:S(2)}) collective-permute-start(bf16[512,2,3,2,16]{0,4,3,2,1:T(8,128)(2,1)S(1)} %slice.148), channel_id=1, source_target_pairs={{0,3},{1,0},{2,1},{3,2},{4,7},{5,4},{6,5},{7,6},{8,11},{9,8},{10,9... | collective-permute-start | bytes 589832 | tf_op jit(solution)/shard_map/ppermute | solution.py:12
  25.2 3.2 %copy-start.13 = (f32[3,2,3,3,2,128]{5,4,3,2,1,0:T(2,128)S(1)}, f32[3,2,3,3,2,128]{5,4,3,2,1,0:T(2,128)}, u32[]{:S(2)}) copy-start(f32[3,2,3,3,2,128]{5,4,3,2,1,0:T(2,128)} %param.5) | copy-start | bytes 165892
  31.9 1.8 copy-start.2
  33.7 2.9 %copy-start.3 = (bf16[512,1536]{1,0:T(8,128)(2,1)S(1)}, bf16[512,1536]{1,0:T(8,128)(2,1)}, u32[]{:S(2)}) copy-start(bf16[512,1536]{1,0:T(8,128)(2,1)} %reshape.106) | copy-start | bytes 4718596
  36.6 3.4 %copy-start.12 = (f32[1,2,3,3,2,128]{5,4,3,2,1,0:T(2,128)S(1)}, f32[1,2,3,3,2,128]{5,4,3,2,1,0:T(2,128)}, u32[]{:S(2)}) copy-start(f32[1,2,3,3,2,128]{5,4,3,2,1,0:T(2,128)} %get-tuple-element.35) | copy-start | bytes 55300
  36.6 4.1 %copy-start.5 = (bf16[512,2,3,2,8,16]{0,5,4,3,2,1:T(8,128)(2,1)S(1)}, bf16[512,2,3,2,8,16]{0,5,4,3,2,1:T(8,128)(2,1)}, u32[]{:S(2)}) copy-start(bf16[512,2,3,2,8,16]{0,5,4,3,2,1:T(8,128)(2,1)} %pad_maximum_fusion.5) | copy-start | bytes 4718596
  36.6 4.1 %copy-start.6 = (bf16[512,2,3,2,112]{0,4,3,2,1:T(8,128)(2,1)S(1)}, bf16[512,2,3,2,112]{0,4,3,2,1:T(8,128)(2,1)}, u32[]{:S(2)}) copy-start(bf16[512,2,3,2,112]{0,4,3,2,1:T(8,128)(2,1)} %slice.147) | copy-start | bytes 4128772
  36.6 4.1 %copy-start.8 = (bf16[512,2,3,1,128]{0,4,3,2,1:T(8,128)(2,1)S(1)}, bf16[512,2,3,1,128]{0,4,3,2,1:T(8,128)(2,1)}, u32[]{:S(2)}) copy-start(bf16[512,2,3,1,128]{0,4,3,2,1:T(8,128)(2,1)} %get-tuple-element.27) | copy-start | bytes 2359300
  46.3 1.9 copy-start.17
  46.3 1.9 copy-start.18
  60.5 3.1 %copy-start.15 = (f32[3,3,2,128]{3,2,1,0:T(2,128)S(1)}, f32[3,3,2,128]{3,2,1,0:T(2,128)}, u32[]{:S(2)}) copy-start(f32[3,3,2,128]{3,2,1,0:T(2,128)} %get-tuple-element.49) | copy-start | bytes 27652
  60.5 3.1 %copy-start.16 = (f32[3,3,2,128]{3,2,1,0:T(2,128)S(1)}, f32[3,3,2,128]{3,2,1,0:T(2,128)}, u32[]{:S(2)}) copy-start(f32[3,3,2,128]{3,2,1,0:T(2,128)} %get-tuple-element.50) | copy-start | bytes 27652
  74.7 5.7 %copy-start.7 = (bf16[1024,1536]{1,0:T(8,128)(2,1)S(1)}, bf16[1024,1536]{1,0:T(8,128)(2,1)}, u32[]{:S(2)}) copy-start(bf16[1024,1536]{1,0:T(8,128)(2,1)} %pad_maximum_fusion.1) | copy-start | bytes 9437188
  74.7 5.7 %copy-start.11 = (bf16[512,1536,1]{1,0,2:T(8,128)(2,1)S(1)}, bf16[512,1536,1]{1,0,2:T(8,128)(2,1)}, u32[]{:S(2)}) copy-start(bf16[512,1536,1]{1,0,2:T(8,128)(2,1)} %reshape.118) | copy-start | bytes 4718596
  85.2 1.7 copy-start.4
  85.2 1.7 copy-start.14
  92.2 3.9 %copy-start.9 = (f32[1,2,512,512]{3,2,1,0:T(8,128)S(1)}, f32[1,2,512,512]{3,2,1,0:T(8,128)}, u32[]{:S(2)}) copy-start(f32[1,2,512,512]{3,2,1,0:T(8,128)} %convolution_bitcast_fusion.2) | copy-start | bytes 6291460
  92.2 3.9 %copy-start.10 = (f32[1,2,512,512]{3,2,1,0:T(8,128)S(1)}, f32[1,2,512,512]{3,2,1,0:T(8,128)}, u32[]{:S(2)}) copy-start(f32[1,2,512,512]{3,2,1,0:T(8,128)} %convolution_bitcast_fusion.1) | copy-start | bytes 6291460
  97.4 4.6 %copy-start = (f32[3,2,512,512]{3,2,1,0:T(8,128)}, f32[3,2,512,512]{3,2,1,0:T(8,128)S(1)}, u32[]{:S(2)}) copy-start(f32[3,2,512,512]{3,2,1,0:T(8,128)S(1)} %maximum_multiply_fusion) | copy-start | bytes 18874372
  116.5 0.8 copy-start.19
Sparse Core Ops, SparseCore 0:
  116.7 111.6 reduce-scatter.1
where the time goes:
time: 247 us; the launch traced here: 246 us
  waiting for transfers between devices  79.9 us (32%)
  local copies, waits for them, and re-layouts  50.1 us (20%)
  blocking collectives  39.7 us (16%)
  other arithmetic  37.9 us (15%)
  between operations  18 us (7%)
  matrix products  13.7 us (6%)
  starting transfers between devices  6.77 us (3%)
    reduce_scatter x1, waiting for transfers between devices, on_device(): lax.psum_scatter(local_terms, ('wide', 'narrow'), scatter_dimension=2, ti...  79.9 us
    all_gather x1, blocking collectives, on_device(): piece = lax.all_gather(peram, 'wide', axis=1, tiled=True)  30.8 us
    mul x8, local copies, waits for them, and re-layouts, covariant_product(): out_real = jnp.sum(link_real * vec_real - link_imag * vec_imag, axis=2)  13.8 us
    dot_general x3, matrix products, on_device(): lax.dot_general(left_block, product, (((1,), (1,)), ((), ())), preferred_...  12.7 us
    unnamed x45, local copies, waits for them, and re-layouts  9.99 us
    all_gather x1, blocking collectives, on_device(): elementals = lax.all_gather(thin_rows, 'narrow', axis=2, tiled=True)  8.85 us
    another operation x2, other arithmetic, on_device(): jnp.stack([real_part - jnp.swapaxes(real_part, 1, 2), imag_part + jnp.swa...  8.68 us
    reduce_sum x3, other arithmetic, covariant_product(): out_real = jnp.sum(link_real * vec_real - link_imag * vec_imag, axis=2)  7.61 us
  transfers between devices with their start and end apart: 3, of which 1 were waited for; matrix products, arithmetic and copies ran while one was open for 7% of the time, Pallas kernels for 0%

commit v1 on v0

--- a/solution.py
+++ b/solution.py
@@ -67,7 +67,12 @@
     elem_low = elementals.astype(jnp.bfloat16)
     real_rows = elem_low[:, 0]
     imag_rows = elem_low[:, 1]
-    piece = lax.all_gather(peram, "wide", axis=1, tiled=True)
+    ring = [peram]
+    for hop in range(7):
+        ring.append(lax.ppermute(ring[-1], "wide", [(dev, (dev + 1) % 8) for dev in range(8)]))
+    piece = jnp.roll(
+        jnp.concatenate(ring[::-1], axis=1), (lax.axis_index("wide") + 1) * ring[0].shape[1], axis=1
+    )
     width = piece.shape[1]
     left_part = jnp.concatenate([real_rows, imag_rows], 2).reshape(-1, 2 * width)
     right_part = jnp.concatenate(

time: 247 us -> 247 us (level)
  waiting for transfers between devices: 79.9 us -> 111 us
  blocking collectives: 39.7 us -> 8.66 us
    ppermute x0 -> x7, waiting for transfers between devices: none -> 46.4 us  [on_device(): lax.ppermute(ring[-1], 'wide', [(dev, (dev + 1) % 8) for dev in range(8)])]
    all_gather x1 -> x0, blocking collectives: 30.8 us -> none  [on_device(): piece = lax.all_gather(peram, 'wide', axis=1, tiled=True)]
    reduce_scatter x1, waiting for transfers between devices: 79.9 us -> 64.1 us  [on_device(): lax.psum_scatter(local_terms, ('wide', 'narrow'), scatter_dimension=2, ti...]
    unnamed x45 -> x60, local copies, waits for them, and re-layouts: 9.99 us -> 10.1 us
  transfers between devices with their start and end apart: 3 -> 10, of which waited for: 1 -> 8; matrix products, arithmetic and copies ran while one was open for 7% -> 7% of each run, Pallas kernels for 0% -> 0%
where the time goes in v1:
time: 247 us; the launch traced here: 246 us
  waiting for transfers between devices  111 us (45%)
  local copies, waits for them, and re-layouts  50.5 us (20%)
  other arithmetic  37.9 us (15%)
  between operations  18.3 us (7%)
  matrix products  13.7 us (6%)
  blocking collectives  8.66 us (4%)
  starting transfers between devices  6.79 us (3%)
    reduce_scatter x1, waiting for transfers between devices, on_device(): lax.psum_scatter(local_terms, ('wide', 'narrow'), scatter_dimension=2, ti...  64.1 us
    ppermute x7, waiting for transfers between devices, on_device(): lax.ppermute(ring[-1], 'wide', [(dev, (dev + 1) % 8) for dev in range(8)])  46.4 us
    mul x8, local copies, waits for them, and re-layouts, covariant_product(): out_real = jnp.sum(link_real * vec_real - link_imag * vec_imag, axis=2)  13.8 us
    dot_general x3, matrix products, on_device(): lax.dot_general(left_block, product, (((1,), (1,)), ((), ())), preferred_...  12.7 us
    unnamed x60, local copies, waits for them, and re-layouts  10.1 us
    another operation x2, other arithmetic, on_device(): jnp.stack([real_part - jnp.swapaxes(real_part, 1, 2), imag_part + jnp.swa...  8.67 us
    all_gather x1, blocking collectives, on_device(): elementals = lax.all_gather(thin_rows, 'narrow', axis=2, tiled=True)  8.66 us
    reduce_sum x3, other arithmetic, covariant_product(): out_real = jnp.sum(link_real * vec_real - link_imag * vec_imag, axis=2)  7.61 us
  transfers between devices with their start and end apart: 10, of which 8 were waited for; matrix products, arithmetic and copies ran while one was open for 7% of the time, Pallas kernels for 0%

profile of v1, /device:TPU:0, one launch (start us, length us, event | category | flops | bytes accessed | tf_op | source)
XLA Modules:
  0.0 246.4 jit_solution(9213583524451780527)
XLA Ops:
  7.2 3.6 %copy.27 = bf16[512,2,3,2,128]{0,4,3,2,1:T(8,128)(2,1)S(1)} copy(bf16[512,2,3,2,128]{4,3,2,1,0:T(2,128)(2,1)} %param.4) | data formatting | bytes 3145728 | tf_op args[0]
  12.1 6.0 %collective-permute-start = (bf16[512,2,3,1,128]{0,4,3,2,1:T(8,128)(2,1)}, bf16[512,2,3,1,128]{0,4,3,2,1:T(8,128)(2,1)}, u32[]{:S(2)}, u32[]{:S(2)}) collective-permute-start(bf16[512,2,3,1,128]{0,4,3,2,1:T(8,128)(2,1)} %get-tuple-element.30), channel_id=1, source_target_pairs={{0,28},{4,0},{8,4},{12,8},{16,12},{20,16},{24,20},{28,24},{1,29},{... | collective-permute-start | bytes 2359304 | tf_op jit(solution)/shard_map/ppermute | solution.py:12
  25.5 3.2 %pad_maximum_fusion.2 = bf16[512,2,3,2,128]{4,3,2,1,0:T(2,128)(2,1)} fusion(bf16[512,1,3,2,128]{4,3,2,1,0:T(2,128)(2,1)S(1)} %get-tuple-element.32, bf16[512,1,3,2,128]{4,3,2,1,0:T(2,128)(2,1)S(1)} %get-tuple-element.31), kind=kLoop, calls=%fused_computation.17 | loop fusion | flops 786432 | bytes 3145728 | tf_op jit(solution)/shard_map/concatenate | solution.py:41
  29.4 1.7 pad_maximum_fusion.5
  37.0 3.4 %pad_maximum_fusion.1 = bf16[1024,1536]{1,0:T(8,128)(2,1)} fusion(bf16[512,1536]{1,0:T(8,128)(2,1)} %reshape.107, bf16[512,1536]{1,0:T(8,128)(2,1)S(1)} %copy-done.3), kind=kLoop, calls=%fused_computation.9 | loop fusion | flops 6291456 | bytes 6291456 | tf_op jit(solution)/shard_map/concatenate | solution.py:42
  41.1 3.5 %fusion.2 = (bf16[512,2,3,2,128]{0,4,3,2,1:T(8,128)(2,1)S(1)}, bf16[512,2,3,2,128]{0,4,3,2,1:T(8,128)(2,1)}, bf16[512,2,3,2,128]{0,4,3,2,1:T(8,128)(2,1)}) fusion(bf16[512,2,3,2,8,16]{0,5,4,3,2,1:T(8,128)(2,1)S(1)} %copy-done.5, pred[]{:T(512)} %bitcast.2, pred[]{:T(512)} %bitcast.1, bf16[512,2,3,2,16]{0,4,3,2,1:T(8,128)(2,1)S(1)} %collective-permute-done.1, ...), kind=kLoop, calls=%fused_computation.27 | loop fusion | flops 11010048 | bytes 9437190 | tf_op jit(solution)/shard_map/jit(_where)/select_n | solution.py:48
  46.7 1.9 copy.33
  53.4 4.4 %fusion.6 = (f32[512,3,2,128]{0,3,2,1:T(8,128)S(1)}, f32[512,3,2,128]{0,3,2,1:T(8,128)S(1)}, f32[512,3,2,128]{0,3,2,1:T(8,128)}, f32[512,3,2,128]{0,3,2,1:T(8,128)}) fusion(bf16[512,2,3,2,128]{0,4,3,2,1:T(8,128)(2,1)} %get-tuple-element.22, bf16[512,2,3,2,128]{0,4,3,2,1:T(8,128)(2,1)} %get-tuple-element.21), kind=kLoop, calls=%fused_computation.34 | loop fusion | flops 1572864 | bytes 9437184 | tf_op jit(solution)/shard_map/mul | solution.py:20
  57.8 3.1 %copy.35 = f32[512,3,2,128]{3,0,2,1:T(8,128)} copy(f32[512,3,2,128]{0,3,2,1:T(8,128)} %get-tuple-element.48) | data formatting | bytes 3145728 | tf_op jit(solution)/shard_map/mul | solution.py:20
  60.9 3.1 %copy.36 = f32[512,3,2,128]{3,0,2,1:T(8,128)} copy(f32[512,3,2,128]{0,3,2,1:T(8,128)} %get-tuple-element.47) | data formatting | bytes 3145728 | tf_op jit(solution)/shard_map/mul | solution.py:20
  64.0 3.3 %subtract_reduce_fusion.1 = (bf16[512,3,2,128]{3,0,2,1:T(8,128)(2,1)S(1)}, bf16[512,3,2,128]{3,0,2,1:T(8,128)(2,1)S(1)}) fusion(f32[512,3,2,128]{3,0,2,1:T(8,128)} %copy.36, f32[3,3,2,128]{3,2,1,0:T(2,128)S(1)} %copy-done.16, f32[512,3,2,128]{3,0,2,1:T(8,128)} %copy.35, f32[3,3,2,128]{3,2,1,0:T(2,128)S(1)} %copy-done.17), kind=kLoop, calls=%fused_computation.5 | loop fusion | flops 8650752 | bytes 4737024 | tf_op jit(solution)/shard_map/reduce_sum | solution.py:20
  67.5 2.8 %copy.37 = bf16[512,2,3,2,128]{4,3,2,1,0:T(2,128)(2,1)} copy(bf16[512,2,3,2,128]{4,0,3,2,1:T(8,128)(2,1)S(1)} %pad_maximum_fusion.7) | data formatting | bytes 3145728 | tf_op jit(solution)/shard_map/stack | solution.py:22
  70.3 4.9 %reshape.118 = bf16[512,1536,1]{1,0,2:T(8,128)(2,1)} reshape(bf16[512,2,3,2,128]{4,3,2,1,0:T(2,128)(2,1)} %copy.37) | data formatting | bytes 3145728 | tf_op jit(solution)/shard_map/convert_element_type | solution.py:22
  75.2 5.7 %convolution_bitcast_fusion.2 = f32[1,2,512,512]{3,2,1,0:T(8,128)} fusion(bf16[2,512,1536]{2,1,0:T(8,128)(2,1)} %bitcast.134, bf16[512,1536,1]{1,0,2:T(8,128)(2,1)} %reshape.117), kind=kOutput, calls=%fused_computation.16 | convolution fusion | flops 1610612736 | bytes 6815744 | tf_op jit(solution)/shard_map/dot_general | solution.py:54
  80.9 3.2 %convolution_bitcast_fusion.1 = f32[1,2,512,512]{3,2,1,0:T(8,128)} fusion(bf16[2,512,1536]{2,1,0:T(8,128)(2,1)S(1)} %bitcast.136, bf16[512,1536,1]{1,0,2:T(8,128)(2,1)S(1)} %copy-done.11), kind=kOutput, calls=%fused_computation.15 | convolution fusion | flops 1610612736 | bytes 6815744 | tf_op jit(solution)/shard_map/dot_general | solution.py:54
  85.7 1.7 copy.39
  87.4 2.8 %subtract_reduce_fusion = (bf16[512,3,2,128]{3,0,2,1:T(8,128)(2,1)S(1)}, bf16[512,3,2,128]{3,0,2,1:T(8,128)(2,1)S(1)}) fusion(f32[512,3,2,128]{3,0,2,1:T(8,128)} %copy.39, f32[3,3,2,128]{3,2,1,0:T(2,128)S(1)} %copy-done.15, f32[512,3,2,128]{3,0,2,1:T(8,128)S(1)} %copy-done.4, f32[3,3,2,128]{3,2,1,0:T(2,128)S(1)} %get-tuple-element.42), kind=kLoop, calls=%fused_computation.3 | loop fusion | flops 8650752 | bytes 4737024 | tf_op jit(solution)/shard_map/reduce_sum | solution.py:20
  92.7 3.9 %convolution_bitcast_fusion = f32[1,2,512,512]{3,2,1,0:T(8,128)S(1)} fusion(bf16[2,512,1536]{2,1,0:T(8,128)(2,1)} %bitcast.135, bf16[512,1536,1]{1,0,2:T(8,128)(2,1)S(1)} %reshape.119), kind=kOutput, calls=%fused_computation.14 | convolution fusion | flops 1610612736 | bytes 6815744 | tf_op jit(solution)/shard_map/dot_general | solution.py:54
  97.8 3.8 %fusion.15 = (f32[3,1,512,512]{3,2,1,0:T(8,128)}, f32[3,512,512]{2,1,0:T(8,128)}) fusion(f32[3,2,512,512]{3,2,1,0:T(8,128)S(1)} %maximum_multiply_fusion), kind=kLoop, calls=%fused_computation.85 | loop fusion | bytes 12582912 | tf_op jit(solution)/shard_map/slice | solution.py:59
  102.4 2.4 copy.43
  104.8 3.5 %copy.47 = f32[3,1,512,512]{2,3,0,1:T(8,128)} copy(f32[3,1,512,512]{3,2,1,0:T(8,128)} %get-tuple-element.18) | data formatting | bytes 6291456
  108.3 5.3 %fusion = (f32[3,1,512,512]{3,2,0,1:T(8,128)S(1)}, f32[3,1,512,512]{3,2,0,1:T(8,128)S(1)}) fusion(f32[3,1,512,512]{2,3,0,1:T(8,128)} %copy.47, f32[3,2,512,512]{3,2,1,0:T(8,128)} %copy-done, f32[3,512,512]{1,2,0:T(8,128)S(1)} %copy.43), kind=kLoop, calls=%fused_computation.11 | loop fusion | flops 1572864 | bytes 18874368 | tf_op jit(solution)/shard_map/stack | solution.py:61
  113.6 3.4 %pad_maximum_fusion = f32[3,2,512,512]{3,2,0,1:T(8,128)} fusion(f32[3,1,512,512]{3,2,0,1:T(8,128)S(1)} %get-tuple-element.17, f32[3,1,512,512]{3,2,0,1:T(8,128)S(1)} %get-tuple-element.16), kind=kLoop, calls=%fused_computation.1 | loop fusion | flops 1572864 | bytes 12582912 | tf_op jit(solution)/shard_map/stack | solution.py:61
  117.7 6.6 %collective-permute-done.2 = bf16[2,64,64]{2,1,0:T(8,128)(2,1)S(1)} collective-permute-done((bf16[2,64,64]{2,1,0:T(8,128)(2,1)S(1)}, bf16[2,64,64]{2,1,0:T(8,128)(2,1)S(1)}, u32[]{:S(2)}, u32[]{:S(2)}) %collective-permute-start.2) | collective-permute-done | bytes 16416 | tf_op jit(solution)/shard_map/ppermute | solution.py:72
  124.3 6.6 %collective-permute-done.3 = bf16[2,64,64]{2,1,0:T(8,128)(2,1)S(1)} collective-permute-done((bf16[2,64,64]{2,1,0:T(8,128)(2,1)S(1)}, bf16[2,64,64]{2,1,0:T(8,128)(2,1)S(1)}, u32[]{:S(2)}, u32[]{:S(2)}) %collective-permute-start.3) | collective-permute-done | bytes 16416 | tf_op jit(solution)/shard_map/ppermute | solution.py:72
  131.0 6.6 %collective-permute-done.4 = bf16[2,64,64]{2,1,0:T(8,128)(2,1)S(1)} collective-permute-done((bf16[2,64,64]{2,1,0:T(8,128)(2,1)S(1)}, bf16[2,64,64]{2,1,0:T(8,128)(2,1)S(1)}, u32[]{:S(2)}, u32[]{:S(2)}) %collective-permute-start.4) | collective-permute-done | bytes 16416 | tf_op jit(solution)/shard_map/ppermute | solution.py:72
  137.6 6.6 %collective-permute-done.5 = bf16[2,64,64]{2,1,0:T(8,128)(2,1)S(1)} collective-permute-done((bf16[2,64,64]{2,1,0:T(8,128)(2,1)S(1)}, bf16[2,64,64]{2,1,0:T(8,128)(2,1)S(1)}, u32[]{:S(2)}, u32[]{:S(2)}) %collective-permute-start.5) | collective-permute-done | bytes 16416 | tf_op jit(solution)/shard_map/ppermute | solution.py:72
  144.2 6.7 %collective-permute-done.6 = bf16[2,64,64]{2,1,0:T(8,128)(2,1)S(1)} collective-permute-done((bf16[2,64,64]{2,1,0:T(8,128)(2,1)S(1)}, bf16[2,64,64]{2,1,0:T(8,128)(2,1)S(1)}, u32[]{:S(2)}, u32[]{:S(2)}) %collective-permute-start.6) | collective-permute-done | bytes 16416 | tf_op jit(solution)/shard_map/ppermute | solution.py:72
  150.9 6.6 %collective-permute-done.7 = bf16[2,64,64]{2,1,0:T(8,128)(2,1)S(1)} collective-permute-done((bf16[2,64,64]{2,1,0:T(8,128)(2,1)S(1)}, bf16[2,64,64]{2,1,0:T(8,128)(2,1)S(1)}, u32[]{:S(2)}, u32[]{:S(2)}) %collective-permute-start.7) | collective-permute-done | bytes 16416 | tf_op jit(solution)/shard_map/ppermute | solution.py:72
  157.5 6.6 %collective-permute-done.8 = bf16[2,64,64]{2,1,0:T(8,128)(2,1)S(1)} collective-permute-done((bf16[2,64,64]{2,1,0:T(8,128)(2,1)S(1)}, bf16[2,64,64]{2,1,0:T(8,128)(2,1)S(1)}, u32[]{:S(2)}, u32[]{:S(2)}) %collective-permute-start.8) | collective-permute-done | bytes 16416 | tf_op jit(solution)/shard_map/ppermute | solution.py:72
  164.7 64.1 %reduce-scatter.2.cloned.1.call-done = f32[3,2,16,512]{3,2,0,1:T(8,128)} async-done(((f32[3,2,512,512]{3,2,0,1:T(8,128)}), f32[3,2,16,512]{3,2,0,1:T(8,128)}) %reduce-scatter.2.cloned.1.call-update) | async-done | bytes 196624 | tf_op jit(solution)/shard_map/reduce_scatter | solution.py:65
  228.9 8.7 %all_gather.3 = f32[3,2,64,512]{3,2,0,1:T(8,128)S(1)} all-gather(f32[3,2,16,512]{3,2,0,1:T(8,128)} %reduce-scatter.2.cloned.1.call-done), channel_id=1, replica_groups=mesh['grp'=1,'wide'=8,'narrow'=4] {'narrow'}, dimensions={2}, use_global_device_ids=true | all-gather | bytes 983040 | tf_op jit(solution)/shard_map/all_gather | solution.py:66
  (102 shorter events, 28.3 us)
Async XLA Ops:
  7.2 221.7 %reduce-scatter.2.cloned.1.call-start = ((), (), s32[]{:S(2)}) async-start(), calls=%async_computation.1 | async-start | bytes 6488064 | tf_op jit(solution)/shard_map/reduce_scatter | solution.py:65
  12.1 7.7 %copy-start.20 = (s32[3]{0:T(128)S(1)}, s32[3]{0:T(128)}, u32[]{:S(2)}) copy-start(s32[3]{0:T(128)} %param.6) | copy-start | bytes 40
  12.1 12.3 %copy-start.1 = (bf16[512,2,3,2,128]{4,3,2,1,0:T(2,128)(2,1)S(1)}, bf16[512,2,3,2,128]{4,3,2,1,0:T(2,128)(2,1)}, u32[]{:S(2)}) copy-start(bf16[512,2,3,2,128]{4,3,2,1,0:T(2,128)(2,1)} %param.4) | copy-start | bytes 4718596
  12.1 28.9 %collective-permute-start = (bf16[512,2,3,1,128]{0,4,3,2,1:T(8,128)(2,1)}, bf16[512,2,3,1,128]{0,4,3,2,1:T(8,128)(2,1)}, u32[]{:S(2)}, u32[]{:S(2)}) collective-permute-start(bf16[512,2,3,1,128]{0,4,3,2,1:T(8,128)(2,1)} %get-tuple-element.30), channel_id=1, source_target_pairs={{0,28},{4,0},{8,4},{12,8},{16,12},{20,16},{24,20},{28,24},{1,29},{... | collective-permute-start | bytes 2359304 | tf_op jit(solution)/shard_map/ppermute | solution.py:12
  18.2 22.8 %collective-permute-start.1 = (bf16[512,2,3,2,16]{0,4,3,2,1:T(8,128)(2,1)S(1)}, bf16[512,2,3,2,16]{0,4,3,2,1:T(8,128)(2,1)S(1)}, u32[]{:S(2)}, u32[]{:S(2)}) collective-permute-start(bf16[512,2,3,2,16]{0,4,3,2,1:T(8,128)(2,1)S(1)} %slice.148), channel_id=1, source_target_pairs={{0,3},{1,0},{2,1},{3,2},{4,7},{5,4},{6,5},{7,6},{8,11},{9,8},{10,9... | collective-permute-start | bytes 589832 | tf_op jit(solution)/shard_map/ppermute | solution.py:12
  25.5 3.3 %copy-start.14 = (f32[3,2,3,3,2,128]{5,4,3,2,1,0:T(2,128)S(1)}, f32[3,2,3,3,2,128]{5,4,3,2,1,0:T(2,128)}, u32[]{:S(2)}) copy-start(f32[3,2,3,3,2,128]{5,4,3,2,1,0:T(2,128)} %param.5) | copy-start | bytes 165892
  32.3 1.8 copy-start.2
  34.1 2.9 %copy-start.3 = (bf16[512,1536]{1,0:T(8,128)(2,1)S(1)}, bf16[512,1536]{1,0:T(8,128)(2,1)}, u32[]{:S(2)}) copy-start(bf16[512,1536]{1,0:T(8,128)(2,1)} %reshape.106) | copy-start | bytes 4718596
  37.0 3.4 %copy-start.13 = (f32[1,2,3,3,2,128]{5,4,3,2,1,0:T(2,128)S(1)}, f32[1,2,3,3,2,128]{5,4,3,2,1,0:T(2,128)}, u32[]{:S(2)}) copy-start(f32[1,2,3,3,2,128]{5,4,3,2,1,0:T(2,128)} %get-tuple-element.35) | copy-start | bytes 55300
  37.0 4.0 %copy-start.5 = (bf16[512,2,3,2,8,16]{0,5,4,3,2,1:T(8,128)(2,1)S(1)}, bf16[512,2,3,2,8,16]{0,5,4,3,2,1:T(8,128)(2,1)}, u32[]{:S(2)}) copy-start(bf16[512,2,3,2,8,16]{0,5,4,3,2,1:T(8,128)(2,1)} %pad_maximum_fusion.5) | copy-start | bytes 4718596
  37.0 4.0 %copy-start.6 = (bf16[512,2,3,2,112]{0,4,3,2,1:T(8,128)(2,1)S(1)}, bf16[512,2,3,2,112]{0,4,3,2,1:T(8,128)(2,1)}, u32[]{:S(2)}) copy-start(bf16[512,2,3,2,112]{0,4,3,2,1:T(8,128)(2,1)} %slice.147) | copy-start | bytes 4128772
  37.0 4.0 %copy-start.8 = (bf16[512,2,3,1,128]{0,4,3,2,1:T(8,128)(2,1)S(1)}, bf16[512,2,3,1,128]{0,4,3,2,1:T(8,128)(2,1)}, u32[]{:S(2)}) copy-start(bf16[512,2,3,1,128]{0,4,3,2,1:T(8,128)(2,1)} %get-tuple-element.29) | copy-start | bytes 2359300
  46.7 1.9 copy-start.18
  46.7 1.9 copy-start.19
  60.9 3.1 %copy-start.16 = (f32[3,3,2,128]{3,2,1,0:T(2,128)S(1)}, f32[3,3,2,128]{3,2,1,0:T(2,128)}, u32[]{:S(2)}) copy-start(f32[3,3,2,128]{3,2,1,0:T(2,128)} %get-tuple-element.49) | copy-start | bytes 27652
  60.9 3.1 %copy-start.17 = (f32[3,3,2,128]{3,2,1,0:T(2,128)S(1)}, f32[3,3,2,128]{3,2,1,0:T(2,128)}, u32[]{:S(2)}) copy-start(f32[3,3,2,128]{3,2,1,0:T(2,128)} %get-tuple-element.50) | copy-start | bytes 27652
  75.2 5.7 %copy-start.7 = (bf16[1024,1536]{1,0:T(8,128)(2,1)S(1)}, bf16[1024,1536]{1,0:T(8,128)(2,1)}, u32[]{:S(2)}) copy-start(bf16[1024,1536]{1,0:T(8,128)(2,1)} %pad_maximum_fusion.1) | copy-start | bytes 9437188
  75.2 5.7 %copy-start.11 = (bf16[512,1536,1]{1,0,2:T(8,128)(2,1)S(1)}, bf16[512,1536,1]{1,0,2:T(8,128)(2,1)}, u32[]{:S(2)}) copy-start(bf16[512,1536,1]{1,0,2:T(8,128)(2,1)} %reshape.118) | copy-start | bytes 4718596
  85.7 1.7 copy-start.4
  85.7 1.7 copy-start.15
  92.6 3.9 %copy-start.9 = (f32[1,2,512,512]{3,2,1,0:T(8,128)S(1)}, f32[1,2,512,512]{3,2,1,0:T(8,128)}, u32[]{:S(2)}) copy-start(f32[1,2,512,512]{3,2,1,0:T(8,128)} %convolution_bitcast_fusion.2) | copy-start | bytes 6291460
  92.7 3.9 %copy-start.10 = (f32[1,2,512,512]{3,2,1,0:T(8,128)S(1)}, f32[1,2,512,512]{3,2,1,0:T(8,128)}, u32[]{:S(2)}) copy-start(f32[1,2,512,512]{3,2,1,0:T(8,128)} %convolution_bitcast_fusion.1) | copy-start | bytes 6291460
  97.8 4.6 %copy-start = (f32[3,2,512,512]{3,2,1,0:T(8,128)}, f32[3,2,512,512]{3,2,1,0:T(8,128)S(1)}, u32[]{:S(2)}) copy-start(f32[3,2,512,512]{3,2,1,0:T(8,128)S(1)} %maximum_multiply_fusion) | copy-start | bytes 18874372
  117.0 0.8 copy-start.12
  117.7 6.6 %collective-permute-start.2 = (bf16[2,64,64]{2,1,0:T(8,128)(2,1)S(1)}, bf16[2,64,64]{2,1,0:T(8,128)(2,1)S(1)}, u32[]{:S(2)}, u32[]{:S(2)}) collective-permute-start(bf16[2,64,64]{2,1,0:T(8,128)(2,1)S(1)} %copy-done.12), channel_id=1, source_target_pairs={{0,4},{4,8},{8,12},{12,16},{16,20},{20,24},{24,28},{28,0},{1,5},{5... | collective-permute-start | bytes 49160 | tf_op jit(solution)/shard_map/ppermute | solution.py:72
  124.3 6.6 %collective-permute-start.3 = (bf16[2,64,64]{2,1,0:T(8,128)(2,1)S(1)}, bf16[2,64,64]{2,1,0:T(8,128)(2,1)S(1)}, u32[]{:S(2)}, u32[]{:S(2)}) collective-permute-start(bf16[2,64,64]{2,1,0:T(8,128)(2,1)S(1)} %collective-permute-done.2), channel_id=1, source_target_pairs={{0,4},{4,8},{8,12},{12,16},{16,20},{20,24},{24,28},{28,0},{1,5},{5... | collective-permute-start | bytes 49160 | tf_op jit(solution)/shard_map/ppermute | solution.py:72
  131.0 6.6 %collective-permute-start.4 = (bf16[2,64,64]{2,1,0:T(8,128)(2,1)S(1)}, bf16[2,64,64]{2,1,0:T(8,128)(2,1)S(1)}, u32[]{:S(2)}, u32[]{:S(2)}) collective-permute-start(bf16[2,64,64]{2,1,0:T(8,128)(2,1)S(1)} %collective-permute-done.3), channel_id=1, source_target_pairs={{0,4},{4,8},{8,12},{12,16},{16,20},{20,24},{24,28},{28,0},{1,5},{5... | collective-permute-start | bytes 49160 | tf_op jit(solution)/shard_map/ppermute | solution.py:72
  137.6 6.6 %collective-permute-start.5 = (bf16[2,64,64]{2,1,0:T(8,128)(2,1)S(1)}, bf16[2,64,64]{2,1,0:T(8,128)(2,1)S(1)}, u32[]{:S(2)}, u32[]{:S(2)}) collective-permute-start(bf16[2,64,64]{2,1,0:T(8,128)(2,1)S(1)} %collective-permute-done.4), channel_id=1, source_target_pairs={{0,4},{4,8},{8,12},{12,16},{16,20},{20,24},{24,28},{28,0},{1,5},{5... | collective-permute-start | bytes 49160 | tf_op jit(solution)/shard_map/ppermute | solution.py:72
  144.2 6.7 %collective-permute-start.6 = (bf16[2,64,64]{2,1,0:T(8,128)(2,1)S(1)}, bf16[2,64,64]{2,1,0:T(8,128)(2,1)S(1)}, u32[]{:S(2)}, u32[]{:S(2)}) collective-permute-start(bf16[2,64,64]{2,1,0:T(8,128)(2,1)S(1)} %collective-permute-done.5), channel_id=1, source_target_pairs={{0,4},{4,8},{8,12},{12,16},{16,20},{20,24},{24,28},{28,0},{1,5},{5... | collective-permute-start | bytes 49160 | tf_op jit(solution)/shard_map/ppermute | solution.py:72
  150.9 6.6 %collective-permute-start.7 = (bf16[2,64,64]{2,1,0:T(8,128)(2,1)S(1)}, bf16[2,64,64]{2,1,0:T(8,128)(2,1)S(1)}, u32[]{:S(2)}, u32[]{:S(2)}) collective-permute-start(bf16[2,64,64]{2,1,0:T(8,128)(2,1)S(1)} %collective-permute-done.6), channel_id=1, source_target_pairs={{0,4},{4,8},{8,12},{12,16},{16,20},{20,24},{24,28},{28,0},{1,5},{5... | collective-permute-start | bytes 49160 | tf_op jit(solution)/shard_map/ppermute | solution.py:72
  157.5 6.6 %collective-permute-start.8 = (bf16[2,64,64]{2,1,0:T(8,128)(2,1)S(1)}, bf16[2,64,64]{2,1,0:T(8,128)(2,1)S(1)}, u32[]{:S(2)}, u32[]{:S(2)}) collective-permute-start(bf16[2,64,64]{2,1,0:T(8,128)(2,1)S(1)} %collective-permute-done.7), channel_id=1, source_target_pairs={{0,4},{4,8},{8,12},{12,16},{16,20},{20,24},{24,28},{28,0},{1,5},{5... | collective-permute-start | bytes 49160 | tf_op jit(solution)/shard_map/ppermute | solution.py:72
Sparse Core Ops, SparseCore 0:
  117.1 111.7 reduce-scatter.1
